TPU v7x, 128 devices: a whole 4x4x4 slice. The times are simulated.
128 devices in a mesh: rows: 64 (over x_lo, y, z, core), feat: 2 (over x_hi).
Axes of the slice: x: 4 (x_hi: 2, x_lo: 2; x = x_hi * 2 + x_lo), y: 4, z: 4, core: 2. Of those that a mesh axis runs over, the one named last changes fastest.
Arguments:
- features: bfloat16 [65536, 256], P('rows', 'feat'), may hold values from -6 to 6
- weight: bfloat16 [256, 256], P('feat'), may hold values from -0.375 to 0.375
- cotangent: bfloat16 [65536, 256], P('rows', 'feat'), may hold values from -6 to 6
- tile_values: bfloat16 [6144, 128, 128], P('rows'), may hold values from -0.15625 to 0.15625
- tile_owner: int32 [6144, 1], P('rows'), may hold values from 0 to 63; in each aligned block of 96 rows (0 to 95, 96 to 191, ...) at most 2 rows name the same one
- tile_block: int32 [6144], P('rows'), may hold values from 0 to 7
- tile_dest: int32 [6144], P('rows'), may hold values from 0 to 7
- node_order: int32 [64, 1024], P('rows'), may hold values from 0 to 1023, each once within a row
Outputs:
- activated: bfloat16 [65536, 256], P('rows', 'feat')
- grad_features: bfloat16 [65536, 256], P('rows', 'feat')
- grad_weight: float32 [256, 256], P('feat')
Inputs may be any that keep to these rules, and one draw needn't show every extreme that they name: `tile_owner`: among the 96 tiles of one device no owning device is named more than 2 times, and some owning device is named exactly 2 times. `node_order`: each row is a permutation of 0 to 1023.
All inputs are finite; a program needn't handle non-finite values.
Results may differ from a plain program's by a relative error of at most 0.0066.
Values may be sent and summed in bfloat16 or wider, within the bound.
A program may use at most 128 MiB of HBM per device.

v0:
```python
import jax
import jax.numpy as jnp
from jax import lax
from jax.sharding import PartitionSpec as P

CAP = 2


def activation(inputs):
    return jax.nn.gelu(inputs, approximate=True)


def local(features, weight, cotangent, tile_values, tile_owner, tile_block, tile_dest, node_order):
    rows_here = features.shape[0]
    feat_width = features.shape[1]
    tile_size = tile_values.shape[1]
    tile_count = tile_values.shape[0]
    peer_count = lax.axis_size("rows")
    blocks_here = rows_here // tile_size
    local_order = node_order[0]
    ordered = features[local_order]
    cot_ordered = cotangent[local_order]
    owners = tile_owner[:, 0]
    owner_hits = (owners[:, None] == jnp.arange(peer_count, dtype=jnp.int32)[None, :]).astype(
        jnp.int32
    )
    slot_rank = jnp.sum((jnp.cumsum(owner_hits, axis=0) - owner_hits) * owner_hits, axis=1)
    flat_slot = owners * CAP + slot_rank
    slot_blocks = (
        jnp.full((peer_count * CAP,), blocks_here, jnp.int32).at[flat_slot].set(tile_block)
    )
    slot_blocks = slot_blocks.reshape(peer_count, CAP)
    dest_hot = (jnp.arange(blocks_here, dtype=jnp.int32)[:, None] == tile_dest[None, :]).astype(
        jnp.float32
    )
    gathered = lax.all_gather(ordered, "rows", axis=0, tiled=True)
    sources = gathered.reshape(-1, tile_size, feat_width)[owners * blocks_here + tile_block]
    fwd_products = jnp.einsum(
        "tij,tjc->tic", tile_values, sources, preferred_element_type=jnp.float32
    )
    summed = jnp.dot(
        dest_hot, fwd_products.reshape(tile_count, -1), precision=lax.Precision.HIGHEST
    )
    aggregated = (ordered.astype(jnp.float32) + summed.reshape(rows_here, feat_width)).astype(
        jnp.bfloat16
    )
    partial_pre = jnp.dot(aggregated, weight, preferred_element_type=jnp.float32)
    preact = lax.psum_scatter(partial_pre, "feat", scatter_dimension=1, tiled=True)
    act_values, pullback = jax.vjp(activation, preact)
    activated_rows = act_values.astype(jnp.bfloat16)
    grad_pre = pullback(cot_ordered.astype(jnp.float32))[0].astype(jnp.bfloat16)
    grad_full = lax.all_gather(grad_pre, "feat", axis=1, tiled=True)
    node_count = rows_here * peer_count
    weight_part = jnp.einsum("rf,rh->fh", aggregated, grad_full, preferred_element_type=jnp.float32)
    grad_weight = lax.psum(weight_part, "rows") * node_count ** (-0.5)
    grad_agg = jnp.einsum(
        "rh,fh->rf", grad_full, weight, preferred_element_type=jnp.float32
    ).astype(jnp.bfloat16)
    dest_rows = grad_agg.reshape(blocks_here, tile_size, feat_width)[tile_dest]
    back_products = jnp.einsum(
        "tji,tjc->tic", tile_values, dest_rows, preferred_element_type=jnp.float32
    )
    outgoing = (
        jnp.zeros((peer_count * CAP, tile_size, feat_width), jnp.float32)
        .at[flat_slot]
        .set(back_products)
    )
    outgoing = outgoing.reshape(peer_count, CAP, tile_size, feat_width)
    incoming, owner_blocks = (
        lax.all_to_all(outgoing, "rows", split_axis=0, concat_axis=0, tiled=True),
        lax.all_to_all(slot_blocks, "rows", split_axis=0, concat_axis=0, tiled=True),
    )
    owner_hot = (
        jnp.arange(blocks_here, dtype=jnp.int32)[:, None] == owner_blocks.reshape(1, -1)
    ).astype(jnp.float32)
    adjoint_sum = jnp.dot(
        owner_hot, incoming.reshape(peer_count * CAP, -1), precision=lax.Precision.HIGHEST
    )
    grad_rows = (grad_agg.astype(jnp.float32) + adjoint_sum.reshape(rows_here, feat_width)).astype(
        jnp.bfloat16
    )
    inverse = (
        jnp.zeros_like(local_order).at[local_order].set(jnp.arange(rows_here, dtype=jnp.int32))
    )
    return (activated_rows[inverse], grad_rows[inverse], grad_weight)


def solution(mesh):
    return jax.shard_map(
        local,
        mesh=mesh,
        in_specs=(
            P("rows", "feat"),
            P("feat", None),
            P("rows", "feat"),
            P("rows", None, None),
            P("rows", None),
            P("rows"),
            P("rows"),
            P("rows", None),
        ),
        out_specs=(P("rows", "feat"), P("rows", "feat"), P("feat", None)),
        check_vma=False,
    )
```

profile of v0, /device:TPU:0, one launch (start us, length us, event | category | flops | bytes accessed | tf_op | source)
XLA Modules:
  0.0 818.6 jit_solution(7184599050233862541)
XLA Ops:
  7.2 0.0 copy-start
  7.2 0.0 all-gather.3.cloned.1.call-start
  7.2 0.8 compare_select_fusion
  8.1 5.1 gather_fusion
  13.2 0.0 all-gather.3.cloned.1.call-update
  13.2 0.0 reduce-scatter.2.cloned.1.call-start
  13.3 0.7 compare_select_fusion.4
  14.0 123.8 %all-gather.3.cloned.1.call-done = bf16[65536,128]{1,0:T(8,128)(2,1)} async-done(((bf16[1024,128]{1,0:T(8,128)(2,1)}), bf16[65536,128]{1,0:T(8,128)(2,1)}) %all-gather.3.cloned.1.call-update) | async-done | bytes 16777232 | tf_op jit(solution)/shard_map/all_gather | solution.py:36
  137.8 8.5 %gather_fusion.1 = bf16[96,128,128]{2,1,0:T(8,128)(2,1)} fusion(bf16[512,128,128]{2,1,0:T(8,128)(2,1)} %bitcast.42, s32[1024]{0:T(1024)S(1)} %pad_clamp_fusion.1), kind=kCustom, calls=%fused_computation.1 | custom fusion | bytes 6291840 | tf_op jit(solution)/shard_map/gather | solution.py:37
  146.2 0.0 copy-done
  146.2 6.9 convolution_bitcast_fusion.1
  153.1 0.0 copy-start.10
  153.1 6.5 copy.17
  159.6 0.0 copy-start.8
  159.6 0.0 copy-start.9
  159.6 0.0 copy-start.3
  159.6 0.0 copy-done.10
  159.7 8.9 %fusion.3 = f32[8,16384]{1,0:T(8,128)} fusion(f32[12,8,128,128]{3,2,1,0:T(8,128)} %bitcast.41, s32[96]{0:T(128)S(1)} %copy-done.10), kind=kOutput, calls=%fused_computation.12 | convolution fusion | flops 150995712 | bytes 6816128 | tf_op jit(solution)/shard_map/dot_general | solution.py:41
  168.6 1.9 reshape.66
  170.5 0.0 copy-done.8
  170.5 2.3 fusion.26
  172.9 0.0 reduce-scatter.2.cloned.1.call-update
  172.9 0.0 copy-done.9
  172.9 0.7 fusion.16
  173.6 0.9 reduce_window_sum.11
  174.5 0.2 select_reduce_fusion
  174.7 1.0 scatter_custom_fusion.1
  175.7 0.8 all_to_all.9
  176.5 6.2 all-to-all-start
  182.7 0.0 copy-done.3
  182.7 4.3 gather_fusion.3
  187.0 9.6 %reduce-scatter.2.cloned.1.call-done = f32[1024,128]{1,0:T(8,128)} async-done(((f32[1024,256]{1,0:T(8,128)}), f32[1024,128]{1,0:T(8,128)}) %reduce-scatter.2.cloned.1.call-update) | async-done | bytes 524304 | tf_op jit(solution)/shard_map/reduce_scatter | solution.py:48
  196.7 2.2 fusion.8
  198.9 10.2 %all_gather.7 = bf16[1024,256]{1,0:T(8,128)(2,1)S(1)} all-gather(bf16[1024,128]{1,0:T(8,128)(2,1)S(1)} %get-tuple-element.3), channel_id=1, replica_groups=mesh['rows'=64,'feat'=2] {'feat'}, dimensions={1}, use_global_device_ids=true | all-gather | bytes 786432 | tf_op jit(solution)/shard_map/all_gather | solution.py:52
  209.1 0.8 copy-done.4
  209.9 0.3 convolution_convert_fusion
  210.2 2.7 gather_fusion.4
  212.9 5.7 convolution_bitcast_fusion
  218.7 6.6 copy.20
  225.2 4.3 broadcast_in_dim.13
  229.5 17.8 %scatter_fusion = f32[128,128,128]{2,1,0:T(8,128)} fusion(f32[128,128,128]{2,1,0:T(8,128)} %broadcast_in_dim.13, s32[96]{0:T(128)S(1)} %fusion.22, f32[96,128,128]{2,1,0:T(8,128)} %copy.20), kind=kCustom, calls=%fused_computation.8 | custom fusion | bytes 18874752 | tf_op jit(solution)/shard_map/scatter | solution.py:66
  247.3 0.0 all-to-all-done
  247.3 0.0 copy-start.2
  247.3 8.3 %all-to-all-start.1 = ((f32[64,2,128,128]{3,2,1,0:T(8,128)}), f32[64,2,128,128]{3,2,1,0:T(8,128)}, u32[]{:S(2)}, u32[]{:S(2)}) async-start(f32[64,2,128,128]{3,2,1,0:T(8,128)} %bitcast.39), calls=%async_computation.2 | async-start | bytes 16777216 | tf_op jit(solution)/shard_map/all_to_all | solution.py:70
  255.7 0.0 all-reduce.2.cloned.1.call-start
  255.8 4.3 scatter_custom_fusion
  260.1 0.0 copy-done.5
  260.1 0.0 copy-done.6
  260.1 0.0 copy-done.7
  260.1 0.9 fusion.25
  261.0 0.0 all-reduce.2.cloned.1.call-update
  261.1 0.5 broadcast.112
  261.6 0.7 reduce.3
  262.3 0.1 eq.48
  262.5 0.0 copy-done.2
  262.5 4.3 gather_fusion.2
  266.8 523.6 %all-reduce.2.cloned.1.call-done = f32[128,256]{1,0:T(8,128)} async-done(((f32[128,256]{1,0:T(8,128)}), f32[128,256]{1,0:T(8,128)}) %all-reduce.2.cloned.1.call-update) | async-done | bytes 131088 | tf_op jit(solution)/shard_map/psum | solution.py:55
  790.3 1.6 broadcast_multiply_fusion
  791.9 0.0 all-to-all-done.1
  791.9 11.4 %fusion = f32[8,16384]{1,0:T(8,128)} fusion(f32[16,8,128,128]{3,2,1,0:T(8,128)} %bitcast.14, s32[128]{0:T(128)S(1)} %eq.48), kind=kOutput, calls=%fused_computation.9 | convolution fusion | flops 201327616 | bytes 8913408 | tf_op jit(solution)/shard_map/dot_general | solution.py:76
  803.3 1.9 reshape.70
  805.3 1.8 add_convert_fusion
  807.0 5.1 gather_fusion.5
  812.1 0.0 copy-done.1
  (12 shorter events, 0.0 us)
Async XLA Ops:
  7.2 139.1 %copy-start = (bf16[96,128,128]{2,1,0:T(8,128)(2,1)S(1)}, bf16[96,128,128]{2,1,0:T(8,128)(2,1)}, u32[]{:S(2)}) copy-start(bf16[96,128,128]{2,1,0:T(8,128)(2,1)} %param.11) | copy-start | bytes 9437188
  7.2 130.6 %all-gather.3.cloned.1.call-start = ((), (), s32[]{:S(2)}) async-start(), calls=%async_computation.5 | async-start | bytes 17039360 | tf_op jit(solution)/shard_map/all_gather | solution.py:36
  13.2 183.4 %reduce-scatter.2.cloned.1.call-start = ((), (), s32[]{:S(2)}) async-start(), calls=%async_computation.3 | async-start | bytes 1572864 | tf_op jit(solution)/shard_map/reduce_scatter | solution.py:48
  153.1 6.5 copy-start.10
  159.6 10.9 %copy-start.8 = (bf16[128,256]{1,0:T(8,128)(2,1)S(1)}, bf16[128,256]{1,0:T(8,128)(2,1)}, u32[]{:S(2)}) copy-start(bf16[128,256]{1,0:T(8,128)(2,1)} %param.9) | copy-start | bytes 196612
  159.6 13.3 %copy-start.9 = (s32[96,1]{0,1:T(1,128)S(1)}, s32[96,1]{0,1:T(1,128)}, u32[]{:S(2)}) copy-start(s32[96,1]{0,1:T(1,128)} %param.12) | copy-start | bytes 1156
  159.6 23.1 %copy-start.3 = (bf16[1024,128]{1,0:T(8,128)(2,1)S(1)}, bf16[1024,128]{1,0:T(8,128)(2,1)}, u32[]{:S(2)}) copy-start(bf16[1024,128]{1,0:T(8,128)(2,1)} %param.10) | copy-start | bytes 786436
  176.5 70.8 %all-to-all-start = ((s32[64,1,2]{2,1,0:T(1,128)}), s32[64,1,2]{2,1,0:T(1,128)S(1)}, u32[]{:S(2)}, u32[]{:S(2)}) async-start(s32[64,1,2]{2,1,0:T(1,128)} %bitcast.7), calls=%async_computation.1 | async-start | bytes 65536 | tf_op jit(solution)/shard_map/all_to_all | solution.py:71
  209.1 0.8 copy-start.4
  247.3 12.8 %copy-start.5 = (bf16[1024,256]{1,0:T(8,128)(2,1)S(1)}, bf16[1024,256]{1,0:T(8,128)(2,1)}, u32[]{:S(2)}) copy-start(bf16[1024,256]{1,0:T(8,128)(2,1)} %copy-done.4) | copy-start | bytes 1572868
  247.3 12.8 %copy-start.6 = (f32[1024,128]{1,0:T(8,128)S(1)}, f32[1024,128]{1,0:T(8,128)}, u32[]{:S(2)}) copy-start(f32[1024,128]{1,0:T(8,128)} %reshape.66) | copy-start | bytes 1572868
  247.3 12.8 %copy-start.7 = (bf16[1024,128]{1,0:T(8,128)(2,1)S(1)}, bf16[1024,128]{1,0:T(8,128)(2,1)}, u32[]{:S(2)}) copy-start(bf16[1024,128]{1,0:T(8,128)(2,1)} %gather_fusion) | copy-start | bytes 786436
  247.3 15.1 %copy-start.2 = (bf16[1024,128]{1,0:T(8,128)(2,1)S(1)}, bf16[1024,128]{1,0:T(8,128)(2,1)}, u32[]{:S(2)}) copy-start(bf16[1024,128]{1,0:T(8,128)(2,1)} %get-tuple-element.4) | copy-start | bytes 786436
  247.3 544.6 %all-to-all-start.1 = ((f32[64,2,128,128]{3,2,1,0:T(8,128)}), f32[64,2,128,128]{3,2,1,0:T(8,128)}, u32[]{:S(2)}, u32[]{:S(2)}) async-start(f32[64,2,128,128]{3,2,1,0:T(8,128)} %bitcast.39), calls=%async_computation.2 | async-start | bytes 16777216 | tf_op jit(solution)/shard_map/all_to_all | solution.py:70
  255.7 534.6 %all-reduce.2.cloned.1.call-start = ((), (), s32[]{:S(2)}) async-start(), calls=%async_computation.4 | async-start | bytes 262144 | tf_op jit(solution)/shard_map/psum | solution.py:55
  791.9 20.2 %copy-start.1 = (bf16[96,128,128]{2,1,0:T(8,128)(2,1)S(1)}, bf16[96,128,128]{2,1,0:T(8,128)(2,1)}, u32[]{:S(2)}) copy-start(bf16[96,128,128]{2,1,0:T(8,128)(2,1)} %param.11) | copy-start | bytes 9437188
Sparse Core Ops, SparseCore 0:
  13.3 124.3 all-gather.2
  173.0 23.5 reduce-scatter.1
  261.2 529.1 all-reduce.1
where the time goes:
time: 820 us; the launch traced here: 819 us
  waiting for transfers between devices  657 us (80%)
  local copies, waits for them, and re-layouts  76.6 us (9%)
  matrix products  36.6 us (4%)
  starting transfers between devices  14.7 us (2%)
  between operations  13.9 us (2%)
  blocking collectives  10.2 us (1%)
  other arithmetic  9.68 us (1%)
    psum x1, waiting for transfers between devices, local(): grad_weight = lax.psum(weight_part, 'rows') * node_count ** (-0.5)  524 us
    all_gather x1, waiting for transfers between devices, local(): gathered = lax.all_gather(ordered, 'rows', axis=0, tiled=True)  124 us
    scatter x1, local copies, waits for them, and re-layouts, local(): outgoing = jnp.zeros((peer_count * CAP, tile_size, feat_width), jnp.float...  17.8 us
  transfers between devices with their start and end apart: 5, of which 3 were waited for; matrix products, arithmetic and copies ran while one was open for 7% of the time, Pallas kernels for 0%

commit v1 on v0

--- a/solution.py
+++ b/solution.py
@@ -1,9 +1,124 @@
 import jax
 import jax.numpy as jnp
 from jax import lax
+from jax.experimental import pallas as pl
+from jax.experimental.pallas import tpu as pltpu
+import functools
 from jax.sharding import PartitionSpec as P
 
 CAP = 2
+MESH = pl.DeviceIdType.MESH
+NS = 120
+
+def ag(G, ssem, rsem, x,y,z,c,f, fwd_partner=True):
+    m4=lambda v: lax.rem(v+4,4)
+    dev=lambda x_,y_,z_,c_: (((x_*4+y_)*4+z_)*2+c_, f)
+    X=1-x
+    A=lambda z_,y_,x_: (((c*4+z_)*4+y_)*2+x_)*3
+    B=lambda y_,z_,x_: 192+(((c*4+y_)*4+z_)*2+x_)*3
+    C1=lambda x_,z_,y_: 384+((c*2+x_)*4+z_)*4+y_
+    C2=lambda x_,y_,z_: 448+((c*2+x_)*4+y_)*4+z_
+    tgt={'x':dev(X,y,z,c),'y+':dev(x,m4(y+1),z,c),'y-':dev(x,m4(y-1),z,c),
+         'z+':dev(x,y,m4(z+1),c),'z-':dev(x,y,m4(z-1),c),'c':dev(x,y,z,1-c)}
+    names={}
+    sent=[]
+    def desc(name,ref_s,ref_d,to):
+        i=names.setdefault(name,len(names))
+        return pltpu.make_async_remote_copy(ref_s,ref_d,ssem.at[i],rsem.at[i],device_id=to,device_id_type=MESH)
+    def view(idx,n,h=None):
+        if h is None: return G.at[pl.ds(idx,n)]
+        return G.at[idx,pl.ds(h*64,64)]
+    def send(name,idx,n,to,h=None):
+        v=view(idx,n,h)
+        d=desc(name,v,v,tgt[to]); d.start(); sent.append(d)
+    def fw(name,idx,n,h=None):
+        if fwd_partner: send('p'+name,idx,n,'c',h); parts.append((name,n,h))
+    parts=[]
+    def wait(name,n,h=None):
+        v=view(0,n,h)
+        desc(name,v,v,tgt['c']).wait_recv()
+    send('Cy+',C1(x,z,y),1,'y+'); send('Cy-',C1(x,z,y),1,'y-')
+    send('Dz+',C2(x,y,z),1,'z+'); send('Dz-',C2(x,y,z),1,'z-')
+    send('Ax',A(z,y,x),3,'x'); send('Bx',B(y,z,x),3,'x')
+    send('Ay+o',A(z,y,x),3,'y+'); send('Ay-o',A(z,y,x),3,'y-')
+    send('Bz+o',B(y,z,x),3,'z+'); send('Bz-o',B(y,z,x),3,'z-')
+    fw('oA',A(z,y,x),3); fw('oB',B(y,z,x),3);
+    yp,ym,y2=m4(y+1),m4(y-1),m4(y+2); zp,zm,z2=m4(z+1),m4(z-1),m4(z+2)
+    wait('Ax',3); send('Ay+x',A(z,y,X),3,'y+'); send('Ay-x',A(z,y,X),3,'y-');
+    wait('Bx',3); send('Bz+x',B(y,z,X),3,'z+'); send('Bz-x',B(y,z,X),3,'z-');
+    wait('Cy+',1); send('Cy+f',C1(x,z,ym),1,'y+',0); wait('Cy-',1); send('Cy-f',C1(x,z,yp),1,'y-',1)
+    wait('Dz+',1); send('Dz+f',C2(x,y,zm),1,'z+',0); wait('Dz-',1); send('Dz-f',C2(x,y,zp),1,'z-',1)
+    send('Az+0',A(z,y,0),6,'z+'); send('Az-0',A(z,y,0),6,'z-')
+    send('By+0',B(y,z,0),6,'y+'); send('By-0',B(y,z,0),6,'y-')
+    fw('Ax',A(z,y,X),3); fw('Bx',B(y,z,X),3)
+    wait('Ay+o',3); wait('Ay-o',3); wait('Ay+x',3); wait('Ay-x',3)
+    send('Ay+f',A(z,ym,0),3,'y+'); send('Ay-f',A(z,yp,1),3,'y-')
+    wait('Bz+o',3); wait('Bz-o',3); wait('Bz+x',3); wait('Bz-x',3)
+    send('Bz+f',B(y,zm,0),3,'z+'); send('Bz-f',B(y,zp,1),3,'z-')
+    wait('Cy+f',1,0); wait('Cy-f',1,1); send('Cz+',C1(x,z,0),4,'z+'); send('Cz-',C1(x,z,0),4,'z-')
+    wait('Dz+f',1,0); wait('Dz-f',1,1); send('Dy+',C2(x,y,0),4,'y+'); send('Dy-',C2(x,y,0),4,'y-')
+    send('Cx0',C1(x,z,0),4,'x'); send('Dx0',C2(x,y,0),4,'x')
+    fw('C0',C1(x,z,0),4); fw('D0',C2(x,y,0),4)
+    for k,yy in ((1,ym),(3,yp)):
+        send(f'Az+{k}',A(z,yy,0),6,'z+'); send(f'Az-{k}',A(z,yy,0),6,'z-')
+        fw(f'Ay{k}',A(z,yy,0),6)
+    for k,zz in ((1,zm),(3,zp)):
+        send(f'By+{k}',B(y,zz,0),6,'y+'); send(f'By-{k}',B(y,zz,0),6,'y-')
+        fw(f'Bz{k}',B(y,zz,0),6)
+    wait('Ay+f',3); wait('Ay-f',3)
+    send('Az+2',A(z,y2,0),6,'z+'); send('Az-2',A(z,y2,0),6,'z-'); fw('Ay2',A(z,y2,0),6)
+    wait('Bz+f',3); wait('Bz-f',3)
+    send('By+2',B(y,z2,0),6,'y+'); send('By-2',B(y,z2,0),6,'y-'); fw('Bz2',B(y,z2,0),6)
+    yk={0:y,1:ym,3:yp,2:y2}; zk={0:z,1:zm,3:zp,2:z2}
+    def bulk(k):
+        wait(f'Az+{k}',6); wait(f'Az-{k}',6)
+        if k in (0,3): send(f'Az+f{k}',A(zm,yk[k],0),6,'z+')
+        else: send(f'Az-f{k}',A(zp,yk[k],0),6,'z-')
+        wait(f'By+{k}',6); wait(f'By-{k}',6)
+        if k in (0,3): send(f'By+f{k}',B(ym,zk[k],0),6,'y+')
+        else: send(f'By-f{k}',B(yp,zk[k],0),6,'y-')
+        fw(f'Azm{k}',A(zm,yk[k],0),6); fw(f'Azp{k}',A(zp,yk[k],0),6)
+        fw(f'Bym{k}',B(ym,zk[k],0),6); fw(f'Byp{k}',B(yp,zk[k],0),6)
+    bulk(0)
+    wait('Cz+',4); wait('Cz-',4); send('Cz+f',C1(x,zm,0),2,'z+'); send('Cz-f',C1(x,zp,2),2,'z-')
+    wait('Dy+',4); wait('Dy-',4); send('Dy+f',C2(x,ym,0),2,'y+'); send('Dy-f',C2(x,yp,2),2,'y-')
+    send('Cxm',C1(x,zm,0),4,'x'); send('Cxp',C1(x,zp,0),4,'x'); send('Dxm',C2(x,ym,0),4,'x'); send('Dxp',C2(x,yp,0),4,'x')
+    fw('Czm',C1(x,zm,0),4); fw('Czp',C1(x,zp,0),4); fw('Dym',C2(x,ym,0),4); fw('Dyp',C2(x,yp,0),4)
+    bulk(1)
+    wait('Cz+f',2); wait('Cz-f',2); send('Cx2',C1(x,z2,0),4,'x'); fw('Cz2',C1(x,z2,0),4)
+    wait('Dy+f',2); wait('Dy-f',2); send('Dx2',C2(x,y2,0),4,'x'); fw('Dy2',C2(x,y2,0),4)
+    bulk(3);
+    wait('Cx0',4); wait('Dx0',4); fw('Cx0',C1(X,z,0),4); fw('Dx0',C2(X,y,0),4)
+    bulk(2)
+    for s,zz,yy in (('m',zm,ym),('p',zp,yp),('2',z2,y2)):
+        wait('Cx'+s,4); fw('Cx'+s,C1(X,zz,0),4); wait('Dx'+s,4); fw('Dx'+s,C2(X,yy,0),4)
+    for k in (0,1,3,2):
+        d='+' if k in (0,3) else '-'
+        wait(f'Az{d}f{k}',6); fw(f'Az2{k}',A(z2,yk[k],0),6)
+        wait(f'By{d}f{k}',6); fw(f'By2{k}',B(y2,zk[k],0),6)
+    for name,n,h in parts: wait('p'+name,n,h)
+    for d in sent: d.wait_send()
+
+def kernel(fwdp, xin, o, G, ssem, rsem, lsem):
+    me=lax.axis_index("rows"); f=lax.axis_index("feat")
+    x=me//32; y=lax.rem(me//8,4); z=lax.rem(me//2,4); c=lax.rem(me,2)
+    m4=lambda v: lax.rem(v+4,4)
+    dev=lambda x_,y_,z_,c_: (((x_*4+y_)*4+z_)*2+c_, f)
+    bar=pltpu.get_barrier_semaphore()
+    for d in (dev(1-x,y,z,c),dev(x,m4(y+1),z,c),dev(x,m4(y-1),z,c),dev(x,y,m4(z+1),c),dev(x,y,m4(z-1),c),dev(x,y,z,1-c)):
+        pl.semaphore_signal(bar,1,device_id=d,device_id_type=MESH)
+    a=(((c*4+z)*4+y)*2+x)*3; b=192+(((c*4+y)*4+z)*2+x)*3; c1=384+((c*2+x)*4+z)*4+y; c2=448+((c*2+x)*4+y)*4+z
+    cps=[pltpu.make_async_copy(xin.at[pl.ds(0,3)],G.at[pl.ds(a,3)],lsem.at[0]),
+         pltpu.make_async_copy(xin.at[pl.ds(3,3)],G.at[pl.ds(b,3)],lsem.at[1]),
+         pltpu.make_async_copy(xin.at[pl.ds(6,1)],G.at[pl.ds(c1,1)],lsem.at[2]),
+         pltpu.make_async_copy(xin.at[pl.ds(7,1)],G.at[pl.ds(c2,1)],lsem.at[3])]
+    for q in cps: q.start()
+    for q in cps: q.wait()
+    pl.semaphore_wait(bar,6)
+    ag(G,ssem,rsem,x,y,z,c,f,fwdp)
+    q=pltpu.make_async_copy(G,o,lsem.at[0])
+    q.start()
+    q.wait()
 
 
 def activation(inputs):
@@ -33,8 +148,21 @@
     dest_hot = (jnp.arange(blocks_here, dtype=jnp.int32)[:, None] == tile_dest[None, :]).astype(
         jnp.float32
     )
-    gathered = lax.all_gather(ordered, "rows", axis=0, tiled=True)
-    sources = gathered.reshape(-1, tile_size, feat_width)[owners * blocks_here + tile_block]
+    gathered = pl.pallas_call(
+        functools.partial(kernel, True),
+        out_shape=jax.ShapeDtypeStruct((512, 128, 128), jnp.bfloat16),
+        in_specs=[pl.BlockSpec(memory_space=pl.ANY)],
+        out_specs=pl.BlockSpec(memory_space=pl.ANY),
+        scratch_shapes=[pltpu.VMEM((512,128,128),jnp.bfloat16),pltpu.SemaphoreType.DMA((NS,)),pltpu.SemaphoreType.DMA((NS,)),pltpu.SemaphoreType.DMA((4,))],
+        compiler_params=pltpu.CompilerParams(collective_id=0,has_side_effects=True,vmem_limit_bytes=60<<20),
+    )(ordered.reshape(8, 128, 128))
+    ox, oy, oz, oc = owners // 32, owners // 8 % 4, owners // 2 % 4, owners % 2
+    fA = (((oc * 4 + oz) * 4 + oy) * 2 + ox) * 3 + tile_block
+    fB = 192 + (((oc * 4 + oy) * 4 + oz) * 2 + ox) * 3 + tile_block - 3
+    fC = 384 + ((oc * 2 + ox) * 4 + oz) * 4 + oy
+    fD = 448 + ((oc * 2 + ox) * 4 + oy) * 4 + oz
+    flat = jnp.where(tile_block < 3, fA, jnp.where(tile_block < 6, fB, jnp.where(tile_block == 6, fC, fD)))
+    sources = gathered[flat]
     fwd_products = jnp.einsum(
         "tij,tjc->tic", tile_values, sources, preferred_element_type=jnp.float32
     )
@@ -61,9 +189,9 @@
         "tji,tjc->tic", tile_values, dest_rows, preferred_element_type=jnp.float32
     )
     outgoing = (
-        jnp.zeros((peer_count * CAP, tile_size, feat_width), jnp.float32)
+        jnp.zeros((peer_count * CAP, tile_size, feat_width), jnp.bfloat16)
         .at[flat_slot]
-        .set(back_products)
+        .set(back_products.astype(jnp.bfloat16))
     )
     outgoing = outgoing.reshape(peer_count, CAP, tile_size, feat_width)
     incoming, owner_blocks = (
@@ -74,7 +202,7 @@
         jnp.arange(blocks_here, dtype=jnp.int32)[:, None] == owner_blocks.reshape(1, -1)
     ).astype(jnp.float32)
     adjoint_sum = jnp.dot(
-        owner_hot, incoming.reshape(peer_count * CAP, -1), precision=lax.Precision.HIGHEST
+        owner_hot.astype(jnp.bfloat16), incoming.reshape(peer_count * CAP, -1), preferred_element_type=jnp.float32
     )
     grad_rows = (grad_agg.astype(jnp.float32) + adjoint_sum.reshape(rows_here, feat_width)).astype(
         jnp.bfloat16

time: 820 us -> 709 us (0.86)
  waiting for transfers between devices: 657 us -> 500 us
  Pallas kernels: 0 us -> 59.5 us
    all_gather x1 -> x0, waiting for transfers between devices: 124 us -> none  [local(): gathered = lax.all_gather(ordered, 'rows', axis=0, tiled=True)]
    pallas_call x0 -> x1, Pallas kernels: none -> 59.5 us  [local(): pl.pallas_call(functools.partial(kernel, True), out_shape=jax.ShapeDtypeS...]
    psum x1, waiting for transfers between devices: 524 us -> 490 us  [local(): grad_weight = lax.psum(weight_part, 'rows') * node_count ** (-0.5)]
  transfers between devices with their start and end apart: 5 -> 4, of which waited for: 3 -> 2; matrix products, arithmetic and copies ran while one was open for 7% -> 8% of each run, Pallas kernels for 0% -> 0%
where the time goes in v1:
time: 709 us; the launch traced here: 708 us
  waiting for transfers between devices  500 us (71%)
  local copies, waits for them, and re-layouts  71 us (10%)
  Pallas kernels  59.5 us (8%)
  matrix products  30.8 us (4%)
  between operations  14.2 us (2%)
  starting transfers between devices  13.4 us (2%)
  blocking collectives  10 us (1%)
  other arithmetic  9.04 us (1%)
    psum x1, waiting for transfers between devices, local(): grad_weight = lax.psum(weight_part, 'rows') * node_count ** (-0.5)  490 us
    pallas_call x1, Pallas kernels, local(): pl.pallas_call(functools.partial(kernel, True), out_shape=jax.ShapeDtypeS...  59.5 us
    scatter x1, local copies, waits for them, and re-layouts, local(): outgoing = jnp.zeros((peer_count * CAP, tile_size, feat_width), jnp.bfloa...  14.6 us
  transfers between devices with their start and end apart: 4, of which 2 were waited for; matrix products, arithmetic and copies ran while one was open for 8% of the time, Pallas kernels for 0%

profile of v1, /device:TPU:0, one launch (start us, length us, event | category | flops | bytes accessed | tf_op | source)
XLA Modules:
  0.0 708.0 jit_solution(13358934872247832941)
XLA Ops:
  7.2 0.0 copy-start
  7.2 0.0 reduce-scatter.2.cloned.1.call-start
  7.2 0.8 compare_select_fusion
  8.1 5.1 gather_fusion
  13.2 0.0 copy-start.4
  13.2 0.0 copy-start.6
  13.2 59.5 %shard_map.103 = bf16[512,128,128]{2,1,0:T(8,128)(2,1)} custom-call(bf16[8,128,128]{2,1,0:T(8,128)(2,1)} %bitcast.39), custom_call_target="tpu_custom_call" | custom-call | tf_op jit(solution)/shard_map/pallas_call | solution.py:151
  72.7 0.0 copy-done.4
  72.7 0.0 copy-done.6
  72.8 8.5 %gather_fusion.1 = bf16[96,128,128]{2,1,0:T(8,128)(2,1)} fusion(bf16[512,128,128]{2,1,0:T(8,128)(2,1)} %shard_map.103, s32[1024]{0:T(1024)S(1)} %pad_clamp_fusion.1), kind=kCustom, calls=%fused_computation.1 | custom fusion | bytes 6291840 | tf_op jit(solution)/shard_map/gather | solution.py:165
  81.2 0.0 copy-done
  81.2 6.9 convolution_bitcast_fusion
  88.1 0.0 copy-start.5
  88.1 6.5 copy.18
  94.7 0.0 copy-done.5
  94.7 0.0 copy-start.3
  94.7 8.9 %fusion = f32[8,16384]{1,0:T(8,128)} fusion(f32[12,8,128,128]{3,2,1,0:T(8,128)} %bitcast.38, s32[96]{0:T(128)S(1)} %copy-done.5), kind=kOutput, calls=%fused_computation.9 | convolution fusion | flops 150995712 | bytes 6816128 | tf_op jit(solution)/shard_map/dot_general | solution.py:169
  103.6 0.0 copy-start.1
  103.6 2.0 reshape.66
  105.6 0.0 copy-done.3
  105.6 2.4 fusion.28
  108.0 0.0 reduce-scatter.2.cloned.1.call-update
  108.0 0.7 fusion.16
  108.7 0.9 reduce_window_sum.11
  109.7 0.2 select_reduce_fusion
  109.8 0.9 scatter_custom_fusion.1
  110.7 0.8 all_to_all.9
  111.5 5.2 all-to-all-start
  116.6 0.0 copy-done.1
  116.7 4.3 gather_fusion.3
  121.0 9.5 %reduce-scatter.2.cloned.1.call-done = f32[1024,128]{1,0:T(8,128)} async-done(((f32[1024,256]{1,0:T(8,128)}), f32[1024,128]{1,0:T(8,128)}) %reduce-scatter.2.cloned.1.call-update) | async-done | bytes 524304 | tf_op jit(solution)/shard_map/reduce_scatter | solution.py:176
  130.5 2.2 fusion.8
  132.7 10.0 %all_gather.3 = bf16[1024,256]{1,0:T(8,128)(2,1)S(1)} all-gather(bf16[1024,128]{1,0:T(8,128)(2,1)S(1)} %get-tuple-element.3), channel_id=1, replica_groups=mesh['rows'=64,'feat'=2] {'feat'}, dimensions={1}, use_global_device_ids=true | all-gather | bytes 786432 | tf_op jit(solution)/shard_map/all_gather | solution.py:180
  142.8 0.0 copy-start.2
  142.8 0.9 copy-done.2
  143.6 0.3 convolution_convert_fusion
  143.9 2.7 gather_fusion.4
  146.7 4.8 convert_bitcast_fusion
  151.5 4.6 copy.21
  156.1 3.0 broadcast_in_dim.13
  159.1 14.6 %scatter_fusion = bf16[128,128,128]{2,1,0:T(8,128)(2,1)} fusion(bf16[128,128,128]{2,1,0:T(8,128)(2,1)} %broadcast_in_dim.13, s32[96]{0:T(128)S(1)} %fusion.24, bf16[96,128,128]{2,1,0:T(8,128)(2,1)} %copy.21), kind=kCustom, calls=%fused_computation.8 | custom fusion | bytes 9437568 | tf_op jit(solution)/shard_map/scatter | solution.py:194
  173.8 0.0 all-to-all-done
  173.8 8.2 %all-to-all-start.1 = ((bf16[64,2,128,128]{3,2,1,0:T(8,128)(2,1)}), bf16[64,2,128,128]{3,2,1,0:T(8,128)(2,1)}, u32[]{:S(2)}, u32[]{:S(2)}) async-start(bf16[64,2,128,128]{3,2,1,0:T(8,128)(2,1)} %bitcast.37), calls=%async_computation.2 | async-start | bytes 8388608 | tf_op jit(solution)/shard_map/all_to_all | solution.py:198
  182.0 0.0 all-reduce.2.cloned.1.call-start
  182.0 4.3 scatter_custom_fusion
  186.3 2.2 fusion.27
  188.5 0.0 all-reduce.2.cloned.1.call-update
  188.6 0.5 broadcast.148
  189.1 0.7 reduce.3
  189.8 0.1 eq.56
  190.0 5.1 gather_fusion.2
  195.0 490.5 %all-reduce.2.cloned.1.call-done = f32[128,256]{1,0:T(8,128)} async-done(((f32[128,256]{1,0:T(8,128)}), f32[128,256]{1,0:T(8,128)}) %all-reduce.2.cloned.1.call-update) | async-done | bytes 131088 | tf_op jit(solution)/shard_map/psum | solution.py:183
  685.5 1.6 broadcast_multiply_fusion
  687.1 0.0 all-to-all-done.1
  687.1 5.3 fusion.3
  692.4 1.9 reshape.70
  694.3 1.8 add_convert_fusion
  696.1 5.1 gather_fusion.5
  (8 shorter events, 0.1 us)
Async XLA Ops:
  7.2 74.1 %copy-start = (bf16[96,128,128]{2,1,0:T(8,128)(2,1)S(1)}, bf16[96,128,128]{2,1,0:T(8,128)(2,1)}, u32[]{:S(2)}) copy-start(bf16[96,128,128]{2,1,0:T(8,128)(2,1)} %param.11) | copy-start | bytes 9437188
  7.2 123.3 %reduce-scatter.2.cloned.1.call-start = ((), (), s32[]{:S(2)}) async-start(), calls=%async_computation.3 | async-start | bytes 1572864 | tf_op jit(solution)/shard_map/reduce_scatter | solution.py:176
  13.2 59.5 %copy-start.4 = (s32[96,1]{0,1:T(1,128)S(1)}, s32[96,1]{0,1:T(1,128)}, u32[]{:S(2)}) copy-start(s32[96,1]{0,1:T(1,128)} %param.12) | copy-start | bytes 1156
  13.2 59.5 %copy-start.6 = (s32[96]{0:T(128)S(1)}, s32[96]{0:T(128)}, u32[]{:S(2)}) copy-start(s32[96]{0:T(128)} %param.13) | copy-start | bytes 1156
  88.1 6.5 copy-start.5
  94.7 10.9 %copy-start.3 = (bf16[128,256]{1,0:T(8,128)(2,1)S(1)}, bf16[128,256]{1,0:T(8,128)(2,1)}, u32[]{:S(2)}) copy-start(bf16[128,256]{1,0:T(8,128)(2,1)} %param.9) | copy-start | bytes 196612
  103.6 13.1 %copy-start.1 = (bf16[1024,128]{1,0:T(8,128)(2,1)S(1)}, bf16[1024,128]{1,0:T(8,128)(2,1)}, u32[]{:S(2)}) copy-start(bf16[1024,128]{1,0:T(8,128)(2,1)} %param.10) | copy-start | bytes 786436
  111.5 62.3 %all-to-all-start = ((s32[64,1,2]{2,1,0:T(1,128)}), s32[64,1,2]{2,1,0:T(1,128)S(1)}, u32[]{:S(2)}, u32[]{:S(2)}) async-start(s32[64,1,2]{2,1,0:T(1,128)} %bitcast.7), calls=%async_computation.1 | async-start | bytes 65536 | tf_op jit(solution)/shard_map/all_to_all | solution.py:199
  142.8 0.9 copy-start.2
  173.8 513.3 %all-to-all-start.1 = ((bf16[64,2,128,128]{3,2,1,0:T(8,128)(2,1)}), bf16[64,2,128,128]{3,2,1,0:T(8,128)(2,1)}, u32[]{:S(2)}, u32[]{:S(2)}) async-start(bf16[64,2,128,128]{3,2,1,0:T(8,128)(2,1)} %bitcast.37), calls=%async_computation.2 | async-start | bytes 8388608 | tf_op jit(solution)/shard_map/all_to_all | solution.py:198
  182.0 503.6 %all-reduce.2.cloned.1.call-start = ((), (), s32[]{:S(2)}) async-start(), calls=%async_computation.4 | async-start | bytes 262144 | tf_op jit(solution)/shard_map/psum | solution.py:183
Sparse Core Ops, SparseCore 0:
  108.1 22.2 reduce-scatter.1
  188.7 496.7 all-reduce.1

commit v2 on v0

v2 whole, which is shorter than its diff:
```python
import jax
import jax.numpy as jnp
from jax import lax
from jax.experimental import pallas as pl
from jax.experimental.pallas import tpu as pltpu
from jax.sharding import PartitionSpec as P

MESH = pl.DeviceIdType.MESH
F32, BF16, I32 = jnp.float32, jnp.bfloat16, jnp.int32
NS = 190
F_TILE, F_SRC, F_DEST, F_CUM, B_TILE, B_DEST, B_BLK = range(7)


class Net:
    def __init__(self, ssem, rsem, targets):
        self.ssem, self.rsem, self.targets = ssem, rsem, targets
        self.names, self.sent = {}, []

    def copy(self, name, src, dst, to):
        i = self.names.setdefault(name, len(self.names))
        return pltpu.make_async_remote_copy(
            src, dst, self.ssem.at[i], self.rsem.at[i], device_id=self.targets[to], device_id_type=MESH
        )

    def send(self, name, src, dst, to):
        d = self.copy(name, src, dst, to)
        d.start()
        self.sent.append(d)

    def wait(self, name, view):
        self.copy(name, view, view, "c").wait_recv()

    def drain(self):
        for d in self.sent:
            d.wait_send()


def gather_blocks(G, net, x, y, z, c, fill):
    m4 = lambda v: lax.rem(v + 4, 4)
    X = 1 - x
    A = lambda z_, y_, x_: (((c * 4 + z_) * 4 + y_) * 2 + x_) * 3
    B = lambda y_, z_, x_: 192 + (((c * 4 + y_) * 4 + z_) * 2 + x_) * 3
    C1 = lambda x_, z_, y_: 384 + ((c * 2 + x_) * 4 + z_) * 4 + y_
    C2 = lambda x_, y_, z_: 448 + ((c * 2 + x_) * 4 + y_) * 4 + z_
    parts = []

    def view(idx, n, h=None):
        if h is None:
            return G.at[pl.ds(idx, n)]
        return G.at[idx, pl.ds(h * 64, 64)]

    def send(name, idx, n, to, h=None):
        v = view(idx, n, h)
        net.send(name, v, v, to)

    def fw(name, idx, n, h=None):
        send("p" + name, idx, n, "c", h)
        parts.append((name, n, h))

    def wait(name, n, h=None):
        net.wait(name, view(0, n, h))

    send('Cy+',C1(x,z,y),1,'y+'); send('Cy-',C1(x,z,y),1,'y-')
    send('Dz+',C2(x,y,z),1,'z+'); send('Dz-',C2(x,y,z),1,'z-')
    send('Ax',A(z,y,x),3,'x'); send('Bx',B(y,z,x),3,'x')
    send('Ay+o',A(z,y,x),3,'y+'); send('Ay-o',A(z,y,x),3,'y-')
    send('Bz+o',B(y,z,x),3,'z+'); send('Bz-o',B(y,z,x),3,'z-')
    fw('oA',A(z,y,x),3); fw('oB',B(y,z,x),3);
    yp,ym,y2=m4(y+1),m4(y-1),m4(y+2); zp,zm,z2=m4(z+1),m4(z-1),m4(z+2)
    wait('Ax',3); send('Ay+x',A(z,y,X),3,'y+'); send('Ay-x',A(z,y,X),3,'y-');
    wait('Bx',3); send('Bz+x',B(y,z,X),3,'z+'); send('Bz-x',B(y,z,X),3,'z-');
    wait('Cy+',1); send('Cy+f',C1(x,z,ym),1,'y+',0); wait('Cy-',1); send('Cy-f',C1(x,z,yp),1,'y-',1)
    wait('Dz+',1); send('Dz+f',C2(x,y,zm),1,'z+',0); wait('Dz-',1); send('Dz-f',C2(x,y,zp),1,'z-',1)
    send('Az+0',A(z,y,0),6,'z+'); send('Az-0',A(z,y,0),6,'z-')
    send('By+0',B(y,z,0),6,'y+'); send('By-0',B(y,z,0),6,'y-')
    fw('Ax',A(z,y,X),3); fw('Bx',B(y,z,X),3)
    wait('Ay+o',3); wait('Ay-o',3); wait('Ay+x',3); wait('Ay-x',3)
    send('Ay+f',A(z,ym,0),3,'y+'); send('Ay-f',A(z,yp,1),3,'y-')
    wait('Bz+o',3); wait('Bz-o',3); wait('Bz+x',3); wait('Bz-x',3)
    send('Bz+f',B(y,zm,0),3,'z+'); send('Bz-f',B(y,zp,1),3,'z-')
    wait('Cy+f',1,0); wait('Cy-f',1,1); send('Cz+',C1(x,z,0),4,'z+'); send('Cz-',C1(x,z,0),4,'z-')
    wait('Dz+f',1,0); wait('Dz-f',1,1); send('Dy+',C2(x,y,0),4,'y+'); send('Dy-',C2(x,y,0),4,'y-')
    send('Cx0',C1(x,z,0),4,'x'); send('Dx0',C2(x,y,0),4,'x')
    fw('C0',C1(x,z,0),4); fw('D0',C2(x,y,0),4)
    fill()
    for k,yy in ((1,ym),(3,yp)):
        send(f'Az+{k}',A(z,yy,0),6,'z+'); send(f'Az-{k}',A(z,yy,0),6,'z-')
        fw(f'Ay{k}',A(z,yy,0),6)
    for k,zz in ((1,zm),(3,zp)):
        send(f'By+{k}',B(y,zz,0),6,'y+'); send(f'By-{k}',B(y,zz,0),6,'y-')
        fw(f'Bz{k}',B(y,zz,0),6)
    fill()
    wait('Ay+f',3); wait('Ay-f',3)
    send('Az+2',A(z,y2,0),6,'z+'); send('Az-2',A(z,y2,0),6,'z-'); fw('Ay2',A(z,y2,0),6)
    wait('Bz+f',3); wait('Bz-f',3)
    send('By+2',B(y,z2,0),6,'y+'); send('By-2',B(y,z2,0),6,'y-'); fw('Bz2',B(y,z2,0),6)
    yk={0:y,1:ym,3:yp,2:y2}; zk={0:z,1:zm,3:zp,2:z2}
    def bulk(k):
        wait(f'Az+{k}',6); wait(f'Az-{k}',6)
        if k in (0,3): send(f'Az+f{k}',A(zm,yk[k],0),6,'z+')
        else: send(f'Az-f{k}',A(zp,yk[k],0),6,'z-')
        wait(f'By+{k}',6); wait(f'By-{k}',6)
        if k in (0,3): send(f'By+f{k}',B(ym,zk[k],0),6,'y+')
        else: send(f'By-f{k}',B(yp,zk[k],0),6,'y-')
        fw(f'Azm{k}',A(zm,yk[k],0),6); fw(f'Azp{k}',A(zp,yk[k],0),6)
        fw(f'Bym{k}',B(ym,zk[k],0),6); fw(f'Byp{k}',B(yp,zk[k],0),6)
    fill()
    bulk(0)
    fill()
    wait('Cz+',4); wait('Cz-',4); send('Cz+f',C1(x,zm,0),2,'z+'); send('Cz-f',C1(x,zp,2),2,'z-')
    wait('Dy+',4); wait('Dy-',4); send('Dy+f',C2(x,ym,0),2,'y+'); send('Dy-f',C2(x,yp,2),2,'y-')
    send('Cxm',C1(x,zm,0),4,'x'); send('Cxp',C1(x,zp,0),4,'x'); send('Dxm',C2(x,ym,0),4,'x'); send('Dxp',C2(x,yp,0),4,'x')
    fw('Czm',C1(x,zm,0),4); fw('Czp',C1(x,zp,0),4); fw('Dym',C2(x,ym,0),4); fw('Dyp',C2(x,yp,0),4)
    fill()
    bulk(1)
    fill()
    wait('Cz+f',2); wait('Cz-f',2); send('Cx2',C1(x,z2,0),4,'x'); fw('Cz2',C1(x,z2,0),4)
    wait('Dy+f',2); wait('Dy-f',2); send('Dx2',C2(x,y2,0),4,'x'); fw('Dy2',C2(x,y2,0),4)
    fill()
    bulk(3)
    fill()
    wait('Cx0',4); wait('Dx0',4); fw('Cx0',C1(X,z,0),4); fw('Dx0',C2(X,y,0),4)
    bulk(2)
    fill()
    for s,zz,yy in (('m',zm,ym),('p',zp,yp),('2',z2,y2)):
        wait('Cx'+s,4); fw('Cx'+s,C1(X,zz,0),4); wait('Dx'+s,4); fw('Dx'+s,C2(X,yy,0),4)
    for k in (0,1,3,2):
        d='+' if k in (0,3) else '-'
        wait(f'Az{d}f{k}',6); fw(f'Az2{k}',A(z2,yk[k],0),6)
        wait(f'By{d}f{k}',6); fw(f'By2{k}',B(y2,zk[k],0),6)
    fill()
    for name,n,h in parts: wait('p'+name,n,h)


def dot(a, b):
    return jnp.dot(a, b, preferred_element_type=F32)


def loop(n, body, unroll):
    def step(i, carry):
        body(i)
        return carry

    lax.fori_loop(0, n, step, 0, unroll=unroll)


def index_tables(pack, TAB):
    owner, block, dest = pack[0:1, :], pack[1:2, :], pack[2:3, :]
    sq = (128, 128)
    row = lambda v: jnp.broadcast_to(v, sq)
    col = lambda v: jnp.broadcast_to(v, sq).T
    i, j = lax.broadcasted_iota(I32, sq, 0), lax.broadcasted_iota(I32, sq, 1)
    count = lambda m: jnp.sum(jnp.where(m, 1, 0), axis=0, keepdims=True)
    co, cd, cb = col(owner), col(dest), col(block)
    rank = count((co == row(owner)) & (i < j))
    place = count((cd < row(dest)) | ((cd == row(dest)) & (i < j)))
    ox, oy, oz, oc = owner >> 5, (owner >> 3) & 3, (owner >> 1) & 3, owner & 1
    fa = (((oc * 4 + oz) * 4 + oy) * 2 + ox) * 3 + block
    fb = 192 + (((oc * 4 + oy) * 4 + oz) * 2 + ox) * 3 + block - 3
    fc = 384 + ((oc * 2 + ox) * 4 + oz) * 4 + oy
    fd = 448 + ((oc * 2 + ox) * 4 + oy) * 4 + oz
    src = jnp.where(block < 3, fa, jnp.where(block < 6, fb, jnp.where(block == 6, fc, fd)))
    op, os = jnp.where(oc == 0, oz, oy), jnp.where(oc == 0, oy, oz)
    slot = (((oc * 4 + op) * 2 + ox) * 4 + os) * 2 + rank
    live = lax.broadcasted_iota(I32, (1, 128), 1) < 96
    slot = jnp.where(live, slot, 999)
    cp, cs = col(place), col(slot)
    pick = lambda m, v: jnp.sum(jnp.where(m, v, 0), axis=0, keepdims=True)
    at_place, at_slot = cp == j, cs == j
    rows = [
        pick(at_place, i),
        pick(at_place, col(src)),
        pick(at_place, cd),
        count((cd <= j) & (i < 96)),
        pick(at_slot, i),
        pick(at_slot, cd),
        pick(at_slot, cb + 1) - 1,
    ]
    for r, (v, most) in enumerate(zip(rows, (95, 511, 7, 96, 95, 7, 7))):
        TAB[r : r + 1, :] = jnp.clip(v, -1 if r == B_BLK else 0, most)


def kernel(
    pack, order, feat, wt, cot, tiles, act_o, gf_o, gw_o,
    G, T, ST, SEG, PM, QM, CO, WO, WR, WOR, COT, AGG, AGO, GP, GA, OS, PP, RP, RL, D, RD, RL2, FX, FR, ACT,
    TAB, TABS, TV, TVS, WG, WZ, W2, WS, W3, WX, W4, WC, WF, ssem, rsem, lsem,
):
    me, f = lax.axis_index("rows"), lax.axis_index("feat")
    x, y, z, c = me // 32, lax.rem(me // 8, 4), lax.rem(me // 2, 4), lax.rem(me, 2)
    p, s = (1 - c) * z + c * y, (1 - c) * y + c * z
    X, e = 1 - x, 1 - c
    m4 = lambda v: lax.rem(v + 4, 4)
    dev = lambda x_, y_, z_, c_: (((x_ * 4 + y_) * 4 + z_) * 2 + c_, f)
    dps = lambda p_, s_, c_: dev(x, (1 - c) * s_ + c * p_, (1 - c) * p_ + c * s_, c_)
    targets = {
        "x": dev(X, y, z, c), "y+": dev(x, m4(y + 1), z, c), "y-": dev(x, m4(y - 1), z, c),
        "z+": dev(x, y, m4(z + 1), c), "z-": dev(x, y, m4(z - 1), c), "c": dev(x, y, z, e), "f": (me, 1 - f),
    }
    for k in (1, 2, 3):
        targets[f"p{k}"], targets[f"s{k}"] = dps(m4(p + k), s, c), dps(p, m4(s + k), c)
        targets[f"P{k}"], targets[f"S{k}"] = dps(m4(p + k), s, e), dps(p, m4(s + k), e)
        targets[f"z{k}"], targets[f"y{k}"] = dev(x, y, m4(z + k), c), dev(x, m4(y + k), z, c)
    entry = lambda r, i, most: jnp.clip(TABS[r, i], 0, most)
    peers = ["x", "f", "c"] + [a + str(k) for a in "psPS" for k in (1, 2, 3)]
    bar = pltpu.get_barrier_semaphore()
    for n in peers:
        pl.semaphore_signal(bar, 1, device_id=targets[n], device_id_type=MESH)
    net = Net(ssem, rsem, targets)
    tile_copy = pltpu.make_async_copy(tiles, T, lsem.at[0])
    tile_copy.start()

    a0, b0 = (((c * 4 + z) * 4 + y) * 2 + x) * 3, 192 + (((c * 4 + y) * 4 + z) * 2 + x) * 3
    c0, d0 = 384 + ((c * 2 + x) * 4 + z) * 4 + y, 448 + ((c * 2 + x) * 4 + y) * 4 + z
    place = [a0, a0 + 1, a0 + 2, b0, b0 + 1, b0 + 2, c0, d0]
    lanes = lax.broadcasted_iota(I32, (128, 1024), 1).astype(F32)
    order_f = order[...].astype(F32)
    for b in range(8):
        oc = jnp.broadcast_to(order_f[:, b * 128 : (b + 1) * 128], (128, 128)).T
        hot = jnp.where(jnp.concatenate([oc] * 8, axis=1) == lanes, 1.0, 0.0).astype(BF16)
        PM[b] = hot
        G[place[b]] = dot(hot, feat[...]).astype(BF16)
    pl.semaphore_wait(bar, len(peers))

    def early():
        net.send("cot", cot, CO, "f")
        net.send("wt", wt, WO, "f")
        index_tables(pack, TAB)
        TV[p * 2 + c] = jnp.broadcast_to(TAB[B_BLK : B_BLK + 1, :], (8, 128))
        q = pltpu.make_async_copy(TAB, TABS, lsem.at[1])
        q.start()
        for k in (1, 2, 3):
            net.send(f"t{k}", TV.at[p * 2 + c], TV.at[p * 2 + c], f"p{k}")
        for k in (0, 1, 2, 3):
            net.send(f"u{k}", TV.at[p * 2 + c], TV.at[s * 2 + c], f"S{k}" if k else "c")
        q.wait()
        tile_copy.wait()

    def transposed(lo):
        def body(i):
            ST[lo + i] = T[entry(B_TILE, lo + i, 95)].T

        return lambda: loop(32, body, 8)

    def weights():
        net.wait("wt", WO)
        for src, dst in ((wt, WR), (WO, WOR)):
            v = src[...]
            u = jnp.concatenate([v[:, 128:], v[:, :128]], axis=1)
            dst[...] = jnp.where(f == 0, v, u)
        net.wait("cot", CO)

    def cotangents():
        def body(b):
            COT[b, :, 0:128] = dot(PM[b], cot[...]).astype(BF16)
            COT[b, :, 128:256] = dot(PM[b], CO[...]).astype(BF16)

        loop(8, body, 1)

    def inverse():
        def body(b):
            j = (lax.broadcasted_iota(I32, (128, 1024), 0) + b * 128).astype(F32)
            QM[b] = jnp.where(jnp.broadcast_to(order_f, (128, 1024)) == j, 1.0, 0.0).astype(BF16)

        loop(8, body, 1)

    def block_tables():
        for k in (1, 2, 3):
            net.wait(f"t{k}", TV.at[0])
        for k in (0, 1, 2, 3):
            net.wait(f"u{k}", TV.at[0])
        q = pltpu.make_async_copy(TV, TVS, lsem.at[1])
        q.start()
        q.wait()

    fillers = [early, transposed(0), transposed(32), transposed(64), transposed(96), weights, cotangents, inverse, block_tables]

    def fill():
        if fillers:
            fillers.pop(0)()

    gather_blocks(G, net, x, y, z, c, fill)
    while fillers:
        fill()

    def product(i, total):
        fresh = (i == 0) | (TABS[F_DEST, i] != TABS[F_DEST, jnp.maximum(i - 1, 0)])
        total = total * jnp.where(fresh, 0.0, 1.0) + dot(T[entry(F_TILE, i, 95)], G[entry(F_SRC, i, 511)])
        SEG[i] = total
        return total

    lax.fori_loop(0, 96, product, jnp.zeros((128, 128), F32), unroll=8)
    for b in range(8):
        last = TABS[F_CUM, b]
        first = TABS[F_CUM, b - 1] if b else 0
        some = jnp.where(last > first, 1.0, 0.0)
        AGG[b] = (G[place[b]].astype(F32) + SEG[jnp.clip(last - 1, 0, 95)] * some).astype(BF16)
        net.send(f"agg{b}", AGG.at[b], AGO.at[b], "f")

    for b in range(8):
        net.wait(f"agg{b}", AGO.at[b])
        own = AGG[b]
        v = dot(own, WR[...]) + dot(AGO[b], WOR[...])
        t = jnp.tanh(0.7978845608 * (v + 0.044715 * (v * v * v)))
        half = 0.5 * (1.0 + t)
        ACT[b] = (v[:, :128] * half[:, :128]).astype(BF16)
        slope = half + 0.5 * v * (1.0 - t * t) * (0.7978845608 * (1.0 + 0.134145 * (v * v)))
        gp = (COT[b].astype(F32) * slope).astype(BF16)
        GA[b] = lax.dot_general(gp, WR[...], (((1,), (1,)), ((), ())), preferred_element_type=F32).astype(BF16)
        part = dot(own.T, gp)
        for q in range(4):
            rows = part[q * 32 : (q + 1) * 32]
            WG[q] = rows if b == 0 else WG[q] + rows

    for k in (1, 2, 3):
        net.send(f"wp{k}", WG.at[m4(z + k)], WZ.at[z], f"z{k}")

    def weight_1():
        for k in (1, 2, 3):
            net.wait(f"wp{k}", WZ.at[0])
        total = WG[z] + WZ[m4(z + 1)] + WZ[m4(z + 2)] + WZ[m4(z + 3)]
        for q in range(4):
            W2[q] = total[q * 8 : (q + 1) * 8]
        for k in (1, 2, 3):
            net.send(f"ws{k}", W2.at[m4(y + k)], WS.at[y], f"y{k}")

    def weight_2():
        for k in (1, 2, 3):
            net.wait(f"ws{k}", WS.at[0])
        W3[...] = W2[y] + WS[m4(y + 1)] + WS[m4(y + 2)] + WS[m4(y + 3)]
        net.send("wx", W3, WX, "x")

    def weight_3():
        net.wait("wx", WX)
        W4[...] = W3[...] + WX[...]
        net.send("wc", W4, WC, "c")

    def weight_4():
        net.wait("wc", WC)
        WF[z, y] = W4[...] + WC[...]
        for k in (1, 2, 3):
            net.send(f"wt{k}", WF.at[z, y], WF.at[z, y], f"y{k}")

    def weight_5():
        for k in (1, 2, 3):
            net.wait(f"wt{k}", WF.at[0, 0])
        for k in (1, 2, 3):
            net.send(f"wq{k}", WF.at[z], WF.at[z], f"z{k}")

    pp, ps = s, p

    def products(plane, p_, h, out):
        base = ((plane * 4 + p_) * 2 + h) * 8

        def body(i):
            out[i // 2, lax.rem(i, 2)] = dot(ST[base + i], GA[entry(B_DEST, base + i, 7)]).astype(BF16)

        loop(8, body, 8)

    def slab(h, k, own):
        q = m4(p + k)
        return (RP if k == 0 else PP).at[q, h]

    for tag, h in (("X", X), ("x", x)):
        for k in (2, 1, 3, 0):
            q, mine = m4(pp + k), m4(p + k)
            products(e, q, h, OS.at[q, h])
            net.send(f"i{tag}{k}", OS.at[q, h], (RP if k == 0 else PP).at[q, h, c], "c")
            products(c, mine, h, slab(h, k, True).at[c])
        for k in (2, 1, 3, 0):
            v = slab(h, k, True)
            net.wait(f"i{tag}{k}", v.at[0])
            if k == 2:
                net.send(f"r+{tag}", v.at[0], RL.at[0, h], "p1")
                net.send(f"r-{tag}", v.at[1], RL.at[1, h], "p3")
            elif k:
                net.send(f"d{k}{tag}", v, RP.at[p, h], f"p{k}")

    def forward_p(tag, h):
        net.wait(f"r+{tag}", RL.at[0, 0])
        net.send(f"g+{tag}", RL.at[0, h], RP.at[m4(p - 1), h, 0], "p1")
        net.wait(f"r-{tag}", RL.at[0, 0])
        net.send(f"g-{tag}", RL.at[1, h], RP.at[m4(p + 1), h, 1], "p3")

    def wait_p(tag):
        for k in (1, 3):
            net.wait(f"d{k}{tag}", RP.at[0, 0])
        net.wait(f"g+{tag}", RP.at[0, 0, 0])
        net.wait(f"g-{tag}", RP.at[0, 0, 0])

    def combine(tag, h):
        def owner(s_):
            q = (((c * 4 + p) * 2 + h) * 4 + s_) * 2
            marks = [[TVS[n, 0, q + r] for r in (0, 1)] for n in range(8)]
            weights_ = [
                [[jnp.where(marks[n][r] == b, 1.0, 0.0) for b in range(8)] for r in (0, 1)] for n in range(8)
            ]

            def chunk(i, carry):
                at = pl.ds(i * 16, 16)
                sums = [jnp.zeros((16, 128), F32) for _ in range(8)]
                for n in range(8):
                    for r in (0, 1):
                        v = RP[n // 2, h, n % 2, s_, r, at, :].astype(F32)
                        sums = [t + v * weights_[n][r][b] for b, t in enumerate(sums)]
                for b in range(8):
                    D[s_, h, b, at, :] = sums[b].astype(BF16)
                return carry

            lax.fori_loop(0, 8, chunk, 0)

        for k in (2, 1, 3, 0):
            owner(m4(s + k))
            v = D.at[m4(s + k), h]
            if k == 2:
                net.send(f"R+{tag}", v.at[pl.ds(0, 4)], RL2.at[0, h], "s1")
                net.send(f"R-{tag}", v.at[pl.ds(4, 4)], RL2.at[1, h], "s3")
            elif k:
                net.send(f"D{k}{tag}", v, RD.at[s, h], f"s{k}")

    def forward_s(tag, h):
        net.wait(f"R+{tag}", RL2.at[0, 0])
        net.send(f"G+{tag}", RL2.at[0, h], RD.at[m4(s - 1), h, pl.ds(0, 4)], "s1")
        net.wait(f"R-{tag}", RL2.at[0, 0])
        net.send(f"G-{tag}", RL2.at[1, h], RD.at[m4(s + 1), h, pl.ds(4, 4)], "s3")

    def wait_s(tag):
        for k in (1, 3):
            net.wait(f"D{k}{tag}", RD.at[0, 0])
        net.wait(f"G+{tag}", RL2.at[0, 0])
        net.wait(f"G-{tag}", RL2.at[0, 0])

    def sum_s(h, b):
        total = D[s, h, b].astype(F32)
        for k in (1, 2, 3):
            total = total + RD[m4(s + k), h, b].astype(F32)
        return total

    forward_p("X", X)
    weight_1()
    for b in range(8):
        rows = jnp.zeros((128, 128), F32)
        for q in range(8):
            rows = rows + dot(QM[b, :, q * 128 : (q + 1) * 128], ACT[q])
        act_o[b * 128 : (b + 1) * 128, :] = rows.astype(BF16)
    wait_p("X")
    combine("X", X)
    weight_2()
    forward_p("x", x)
    forward_s("X", X)
    weight_3()
    wait_s("X")
    for b in range(8):
        FX[b] = sum_s(X, b).astype(BF16)
    net.send("fx", FX, FR, "x")
    wait_p("x")
    combine("x", x)
    weight_4()
    forward_s("x", x)
    weight_5()
    net.wait("fx", FR)
    wait_s("x")
    for b in range(8):
        GP[b] = (GA[b].astype(F32) + FR[b].astype(F32) + sum_s(x, b)).astype(BF16)
    for b in range(8):
        rows = jnp.zeros((128, 128), F32)
        for q in range(8):
            rows = rows + dot(QM[b, :, q * 128 : (q + 1) * 128], GP[q])
        gf_o[b * 128 : (b + 1) * 128, :] = rows.astype(BF16)
    for k in (1, 2, 3):
        net.wait(f"wq{k}", WF.at[0])
    for q in range(16):
        v = WF[q // 4, q % 4] * (65536.0**-0.5)
        u = jnp.concatenate([v[:, 128:], v[:, :128]], axis=1)
        gw_o[q * 8 : (q + 1) * 8, :] = jnp.where(f == 0, v, u)
    net.drain()


def local(features, weight, cotangent, tile_values, tile_owner, tile_block, tile_dest, node_order):
    pack = jnp.stack([tile_owner[:, 0], tile_block, tile_dest])
    pack = jnp.pad(pack, ((0, 5), (0, 32)), constant_values=200)
    vm, hbm = pl.BlockSpec(memory_space=pltpu.VMEM), pl.BlockSpec(memory_space=pl.ANY)
    V = pltpu.VMEM
    tile = (128, 128)
    return pl.pallas_call(
        kernel,
        name="graph_layer",
        out_shape=(
            jax.ShapeDtypeStruct((1024, 128), BF16),
            jax.ShapeDtypeStruct((1024, 128), BF16),
            jax.ShapeDtypeStruct((128, 256), F32),
        ),
        in_specs=[vm, vm, vm, vm, vm, hbm],
        out_specs=(vm, vm, vm),
        scratch_shapes=[
            V((512,) + tile, BF16), V((96,) + tile, BF16), V((128,) + tile, BF16), V((96,) + tile, F32),
            V((8, 128, 1024), BF16), V((8, 128, 1024), BF16), V((1024, 128), BF16), V((128, 256), BF16),
            V((128, 256), BF16), V((128, 256), BF16), V((8, 128, 256), BF16),
            V((8,) + tile, BF16), V((8,) + tile, BF16), V((8,) + tile, BF16), V((8,) + tile, BF16),
            V((4, 2, 4, 2) + tile, BF16), V((4, 2, 2, 4, 2) + tile, BF16), V((4, 2, 2, 4, 2) + tile, BF16),
            V((2, 2, 4, 2) + tile, BF16), V((4, 2, 8) + tile, BF16), V((4, 2, 8) + tile, BF16),
            V((2, 2, 4) + tile, BF16), V((8,) + tile, BF16), V((8,) + tile, BF16), V((8,) + tile, BF16),
            V((16, 128), I32), pltpu.SMEM((16, 128), I32), V((8, 8, 128), I32), pltpu.SMEM((8, 8, 128), I32),
            V((4, 32, 256), F32), V((4, 32, 256), F32), V((4, 8, 256), F32), V((4, 8, 256), F32),
            V((8, 256), F32), V((8, 256), F32), V((8, 256), F32), V((8, 256), F32), V((4, 4, 8, 256), F32),
            pltpu.SemaphoreType.DMA((NS,)), pltpu.SemaphoreType.DMA((NS,)), pltpu.SemaphoreType.DMA((2,)),
        ],
        compiler_params=pltpu.CompilerParams(collective_id=0, has_side_effects=True, vmem_limit_bytes=63 << 20),
    )(pack, node_order, features, weight, cotangent, tile_values)


def solution(mesh):
    return jax.shard_map(
        local,
        mesh=mesh,
        in_specs=(
            P("rows", "feat"), P("feat", None), P("rows", "feat"), P("rows", None, None),
            P("rows", None), P("rows"), P("rows"), P("rows", None),
        ),
        out_specs=(P("rows", "feat"), P("rows", "feat"), P("feat", None)),
        check_vma=False,
    )
```

time: 820 us -> 128 us (0.16)
  waiting for transfers between devices: 657 us -> 0 us
  Pallas kernels: 0 us -> 121 us
  local copies, waits for them, and re-layouts: 76.6 us -> 5.5 us
  matrix products: 36.6 us -> 0 us
  starting transfers between devices: 14.7 us -> 0 us
  between operations: 13.9 us -> 0.64 us
  blocking collectives: 10.2 us -> 0 us
  other arithmetic: 9.68 us -> 0.7 us
    psum x1 -> x0, waiting for transfers between devices: 524 us -> none  [local(): grad_weight = lax.psum(weight_part, 'rows') * node_count ** (-0.5)]
    all_gather x1 -> x0, waiting for transfers between devices: 124 us -> none  [local(): gathered = lax.all_gather(ordered, 'rows', axis=0, tiled=True)]
    pallas_call x0 -> x1, Pallas kernels: none -> 121 us  [local(): pl.pallas_call(kernel, name='graph_layer', out_shape=(jax.ShapeDtypeStruc...]
    dot_general x7 -> x0, matrix products: 36.6 us -> none  [the longest x1 11.4 us: local(): jnp.dot(owner_hot, incoming.reshape(peer_count * CAP, -1), precision=lax....]
    gather x6 -> x0, local copies, waits for them, and re-layouts: 30 us -> none  [the longest x2 9.38 us: local(): return (activated_rows[inverse], grad_rows[inverse], grad_weight)]
    scatter x3 -> x0, local copies, waits for them, and re-layouts: 23.1 us -> none  [the longest x1 17.8 us: local(): outgoing = jnp.zeros((peer_count * CAP, tile_size, feat_width), jnp.float...]
    all_to_all x2 -> x0, starting transfers between devices: 14.5 us -> none  [the longest x1 8.35 us: local(): lax.all_to_all(outgoing, 'rows', split_axis=0, concat_axis=0, tiled=True)]
    dot_general x2 -> x0, local copies, waits for them, and re-layouts: 13.1 us -> none  [the longest x1 6.57 us: local(): jnp.einsum('tji,tjc->tic', tile_values, dest_rows, preferred_element_type...]
  transfers between devices with their start and end apart: 5 -> 0, of which waited for: 3 -> 0; matrix products, arithmetic and copies ran while one was open for 7% -> 0% of each run, Pallas kernels for 0% -> 0%
where the time goes in v2:
time: 128 us
  Pallas kernels  121 us (95%)
  local copies, waits for them, and re-layouts  5.5 us (4%)
    pallas_call x1, Pallas kernels, local(): pl.pallas_call(kernel, name='graph_layer', out_shape=(jax.ShapeDtypeStruc...  121 us
    unnamed x3, local copies, waits for them, and re-layouts  4.91 us

profile of v2, /device:TPU:0, one launch (start us, length us, event | category | flops | bytes accessed | tf_op | source)
XLA Modules:
  0.0 128.0 jit_solution(17921316485665585678)
XLA Ops:
  0.6 0.7 pad_add_fusion
  1.3 0.6 pad.4.pack
  1.9 121.1 %graph_layer.1 = (bf16[1024,128]{1,0:T(8,128)(2,1)}, bf16[1024,128]{1,0:T(8,128)(2,1)}, f32[128,256]{1,0:T(8,128)}) custom-call(s32[8,128]{1,0:T(8,128)} %pad.4.pack, s32[1,1024]{1,0:T(1,128)} %order.1, bf16[1024,128]{1,0:T(8,128)(2,1)} %feat.1, bf16[128,256]{1,0:T(8,128)(2,1)} %wt.1, bf16[1024,128]{1,0:T(8,128)(2,1)} %cot.1, bf16[96,128,128]{2,1,0:T(8,128)(2,1)} %tiles.1), custom_call_target="tpu_custom_call" | custom-call | tf_op jit(solution)/shard_map/graph_layer/pallas_call | solution.py:484
  123.1 1.7 %copy.14 = bf16[1024,128]{1,0:T(8,128)(2,1)} copy(bf16[1024,128]{1,0:T(8,128)(2,1)} %get-tuple-element.6) | data formatting | bytes 524288
  124.8 1.7 %copy.15 = bf16[1024,128]{1,0:T(8,128)(2,1)} copy(bf16[1024,128]{1,0:T(8,128)(2,1)} %get-tuple-element.7) | data formatting | bytes 524288
  126.4 1.6 %copy.16 = f32[128,256]{1,0:T(8,128)} copy(f32[128,256]{1,0:T(8,128)} %get-tuple-element.8) | data formatting | bytes 262144

commit v3 on v2

--- a/solution.py
+++ b/solution.py
@@ -183,7 +183,7 @@
 def kernel(
     pack, order, feat, wt, cot, tiles, act_o, gf_o, gw_o,
     G, T, ST, SEG, PM, QM, CO, WO, WR, WOR, COT, AGG, AGO, GP, GA, OS, PP, RP, RL, D, RD, RL2, FX, FR, ACT,
-    TAB, TABS, TV, TVS, WG, WZ, W2, WS, W3, WX, W4, WC, WF, ssem, rsem, lsem,
+    TAB, TABS, TV, NT, NTS, CP, RS, WG, WZ, W2, WS, W3, WX, W4, WC, WF, ssem, rsem, lsem,
 ):
     me, f = lax.axis_index("rows"), lax.axis_index("feat")
     x, y, z, c = me // 32, lax.rem(me // 8, 4), lax.rem(me // 2, 4), lax.rem(me, 2)
@@ -268,7 +268,20 @@
             net.wait(f"t{k}", TV.at[0])
         for k in (0, 1, 2, 3):
             net.wait(f"u{k}", TV.at[0])
-        q = pltpu.make_async_copy(TV, TVS, lsem.at[1])
+        odd = lax.rem(lax.broadcasted_iota(I32, (8, 128), 1), 2)
+        row = lax.broadcasted_iota(I32, (8, 128), 0)
+        keys = []
+        for n in range(8):
+            k = jnp.where(TV[n] < 0, 8, TV[n]) * 16 + (2 * n + odd)
+            keys += [k, jnp.where(odd == 0, pltpu.roll(k, 127, 1), pltpu.roll(k, 1, 1))]
+        one = lambda m: jnp.where(m, 1, 0)
+        low, high, ends = (jnp.zeros((8, 128), I32) for _ in range(3))
+        for k in keys:
+            at = sum(one(o < k) for o in keys)
+            low, high = low + jnp.where(at == row, k, 0), high + jnp.where(at == row + 8, k, 0)
+            ends = ends + one(k < (row + 1) * 16)
+        NT[0:8, :], NT[8:16, :], NT[16:24, :] = low, high, ends
+        q = pltpu.make_async_copy(NT, NTS, lsem.at[1])
         q.start()
         q.wait()
 
@@ -390,23 +403,22 @@
     def combine(tag, h):
         def owner(s_):
             q = (((c * 4 + p) * 2 + h) * 4 + s_) * 2
-            marks = [[TVS[n, 0, q + r] for r in (0, 1)] for n in range(8)]
-            weights_ = [
-                [[jnp.where(marks[n][r] == b, 1.0, 0.0) for b in range(8)] for r in (0, 1)] for n in range(8)
-            ]
-
-            def chunk(i, carry):
-                at = pl.ds(i * 16, 16)
-                sums = [jnp.zeros((16, 128), F32) for _ in range(8)]
-                for n in range(8):
-                    for r in (0, 1):
-                        v = RP[n // 2, h, n % 2, s_, r, at, :].astype(F32)
-                        sums = [t + v * weights_[n][r][b] for b, t in enumerate(sums)]
-                for b in range(8):
-                    D[s_, h, b, at, :] = sums[b].astype(BF16)
-                return carry
-
-            lax.fori_loop(0, 8, chunk, 0)
+            for n in range(16):
+                CP[n] = RP[n // 4, h, (n // 2) % 2, s_, n % 2]
+
+            def step(j, total):
+                k, before = NTS[j, q], NTS[jnp.maximum(j - 1, 0), q]
+                fresh = (j == 0) | ((k >> 4) != (before >> 4))
+                total = total * jnp.where(fresh, 0.0, 1.0) + CP[jnp.clip(k & 15, 0, 15)].astype(F32)
+                RS[j] = total.astype(BF16)
+                return total
+
+            lax.fori_loop(0, 16, step, jnp.zeros((128, 128), F32), unroll=8)
+            for b in range(8):
+                last = NTS[16 + b, q]
+                first = NTS[15 + b, q] if b else 0
+                some = jnp.where(last > first, 1.0, 0.0)
+                D[s_, h, b] = (RS[jnp.clip(last - 1, 0, 15)].astype(F32) * some).astype(BF16)
 
         for k in (2, 1, 3, 0):
             owner(m4(s + k))
@@ -499,7 +511,8 @@
             V((4, 2, 4, 2) + tile, BF16), V((4, 2, 2, 4, 2) + tile, BF16), V((4, 2, 2, 4, 2) + tile, BF16),
             V((2, 2, 4, 2) + tile, BF16), V((4, 2, 8) + tile, BF16), V((4, 2, 8) + tile, BF16),
             V((2, 2, 4) + tile, BF16), V((8,) + tile, BF16), V((8,) + tile, BF16), V((8,) + tile, BF16),
-            V((16, 128), I32), pltpu.SMEM((16, 128), I32), V((8, 8, 128), I32), pltpu.SMEM((8, 8, 128), I32),
+            V((16, 128), I32), pltpu.SMEM((16, 128), I32), V((8, 8, 128), I32),
+            V((24, 128), I32), pltpu.SMEM((24, 128), I32), V((16,) + tile, BF16), V((16,) + tile, BF16),
             V((4, 32, 256), F32), V((4, 32, 256), F32), V((4, 8, 256), F32), V((4, 8, 256), F32),
             V((8, 256), F32), V((8, 256), F32), V((8, 256), F32), V((8, 256), F32), V((4, 4, 8, 256), F32),
             pltpu.SemaphoreType.DMA((NS,)), pltpu.SemaphoreType.DMA((NS,)), pltpu.SemaphoreType.DMA((2,)),

time: 128 us -> 126 us (0.984)
  Pallas kernels: 121 us -> 119 us
    pallas_call x1, Pallas kernels: 121 us -> 119 us  [local(): pl.pallas_call(kernel, name='graph_layer', out_shape=(jax.ShapeDtypeStruc...]
where the time goes in v3:
time: 126 us
  Pallas kernels  119 us (94%)
  local copies, waits for them, and re-layouts  5.5 us (4%)
    pallas_call x1, Pallas kernels, local(): pl.pallas_call(kernel, name='graph_layer', out_shape=(jax.ShapeDtypeStruc...  119 us
    unnamed x3, local copies, waits for them, and re-layouts  4.91 us

profile of v3, /device:TPU:0, one launch (start us, length us, event | category | flops | bytes accessed | tf_op | source)
XLA Modules:
  0.0 125.7 jit_solution(4708459205798675522)
XLA Ops:
  0.6 0.7 pad_add_fusion
  1.3 0.6 pad.4.pack
  1.9 118.8 %graph_layer.1 = (bf16[1024,128]{1,0:T(8,128)(2,1)}, bf16[1024,128]{1,0:T(8,128)(2,1)}, f32[128,256]{1,0:T(8,128)}) custom-call(s32[8,128]{1,0:T(8,128)} %pad.4.pack, s32[1,1024]{1,0:T(1,128)} %order.1, bf16[1024,128]{1,0:T(8,128)(2,1)} %feat.1, bf16[128,256]{1,0:T(8,128)(2,1)} %wt.1, bf16[1024,128]{1,0:T(8,128)(2,1)} %cot.1, bf16[96,128,128]{2,1,0:T(8,128)(2,1)} %tiles.1), custom_call_target="tpu_custom_call" | custom-call | tf_op jit(solution)/shard_map/graph_layer/pallas_call | solution.py:496
  120.8 1.7 %copy.14 = bf16[1024,128]{1,0:T(8,128)(2,1)} copy(bf16[1024,128]{1,0:T(8,128)(2,1)} %get-tuple-element.6) | data formatting | bytes 524288
  122.4 1.7 %copy.15 = bf16[1024,128]{1,0:T(8,128)(2,1)} copy(bf16[1024,128]{1,0:T(8,128)(2,1)} %get-tuple-element.7) | data formatting | bytes 524288
  124.1 1.6 %copy.16 = f32[128,256]{1,0:T(8,128)} copy(f32[128,256]{1,0:T(8,128)} %get-tuple-element.8) | data formatting | bytes 262144
